TPU v7x, 32 devices: a whole 2x2x4 slice. The times are simulated.
32 devices in a mesh: gx: 4 (over y, x), gy: 8 (over z, core).
Axes of the slice: x: 2, y: 2, z: 4, core: 2. Of those that a mesh axis runs over, the one named last changes fastest.
Arguments:
- right_side: float32 [9, 128, 1024], P(None, 'gx', 'gy'), may hold values from -16 to 16
- diag_blocks: float32 [9, 9, 128, 1024], P(None, None, 'gx', 'gy'), may hold values from -0.3 to 6, as said below
- couple_blocks: float32 [9, 9, 128, 1024], P(None, None, 'gx', 'gy'), may hold values from -0.15 to 1.5, as said below
- transmissibility: float32 [4, 128, 1024], P(None, 'gx', 'gy'), may hold values from 0.1 to 0.8
- pressure_weights: float32 [9, 128, 1024], P(None, 'gx', 'gy'), may hold values from 0.2 to 1
- well_mask: int32 [128, 1024], P('gx', 'gy'), may hold values 0 or 1
Outputs:
- solution: float32 [9, 128, 1024], P(None, 'gx', 'gy')
- estimate: float32 [], replicated
Inputs may be any that keep to these rules, and one draw needn't show every extreme that they name: `diag_blocks`: outside the first column, each block has diagonal entries from 4 to 6 and other entries within 0.3 in magnitude (within 0.05 in the first row); the first column is positive. `couple_blocks`: each block has first-column entries from 0.5 to 1.5, other diagonal entries from 0.6 to 1.2, and other entries within 0.15 in magnitude.
All inputs are finite; a program needn't handle non-finite values. No bound on the sum of `well_mask` on one device may be relied on, other than what follows from the above.
Results may differ from a plain program's by a relative error of at most 0.0003.
Values sent between devices are 32-bit elements; how exact they have to be, the bound alone decides.
A program may use at most 64 MiB of HBM per device.

v0:
```python
import jax
import jax.numpy as jnp
from jax import lax
from jax.sharding import PartitionSpec as P

NC = 9
GSTEPS = 2
LEVELS = 3
COARSE_SWEEPS = 6


relax_factor = 0.8
well_boost = 8.0


def padded_2(shard, sides, width):
    for axis, dim in sides:
        peers, length = (lax.axis_size(axis), shard.shape[dim])
        up = [(i, (i + 1) % peers) for i in range(peers - 1)]
        down = [(j, i) for i, j in up]
        last = lax.slice_in_dim(shard, length - width, length, axis=dim)
        initial = lax.slice_in_dim(shard, 0, width, axis=dim)
        before = lax.ppermute(last, axis, up)
        after = lax.ppermute(initial, axis, down)
        shard = jnp.concatenate([before, shard, after], axis=dim)
    return shard


def four_sides(padded):
    return (
        padded[..., 2:, 1:-1],
        padded[..., :-2, 1:-1],
        padded[..., 1:-1, 2:],
        padded[..., 1:-1, :-2],
    )


def block_padder(values):
    return padded_2(values, (("gx", 1), ("gy", 2)), 1)


def level_padder(values):
    return padded_2(values, (("gx", 0), ("gy", 1)), 1)


def apply_blocks(vector, eff_diag, couple_blocks, face_trans, padder):
    product = jnp.sum(couple_blocks * vector[None], axis=1)
    east_side, west_side, north_side, south_side = four_sides(padder(product))
    own_term = jnp.sum(eff_diag * vector[None], axis=1)
    return own_term - (
        face_trans[0] * east_side
        + face_trans[1] * west_side
        + face_trans[2] * north_side
        + face_trans[3] * south_side
    )


def level_apply(values, coeffs, padder):
    east_side, west_side, north_side, south_side = four_sides(padder(values))
    return coeffs[0] * values + (
        coeffs[1] * east_side
        + coeffs[2] * west_side
        + coeffs[3] * north_side
        + coeffs[4] * south_side
    )


def jacobi_sweep(iterate, source, coeffs, padder):
    return iterate + relax_factor * (source - level_apply(iterate, coeffs, padder)) / coeffs[0]


def coarse_sweeps(source, coeffs, padder):
    iterate = relax_factor * source / coeffs[0]
    for sweep_no in range(COARSE_SWEEPS - 1):
        iterate = jacobi_sweep(iterate, source, coeffs, padder)
    return iterate


def coarsen(coeffs):
    extent_x, extent_y = (coeffs.shape[1], coeffs.shape[2])
    grouped = coeffs.reshape(5, extent_x // 2, 2, extent_y // 2, 2)
    center_fine, east_fine, west_fine, north_fine, south_fine = (
        grouped[0],
        grouped[1],
        grouped[2],
        grouped[3],
        grouped[4],
    )
    center = (
        center_fine.sum(axis=(1, 3))
        + east_fine[:, 0].sum(axis=2)
        + west_fine[:, 1].sum(axis=2)
        + north_fine[:, :, :, 0].sum(axis=1)
        + south_fine[:, :, :, 1].sum(axis=1)
    )
    east_link = east_fine[:, 1].sum(axis=2)
    west_link = west_fine[:, 0].sum(axis=2)
    north_link = north_fine[:, :, :, 1].sum(axis=1)
    south_link = south_fine[:, :, :, 0].sum(axis=1)
    return jnp.stack([center, east_link, west_link, north_link, south_link])


def restrict(values):
    extent_x, extent_y = values.shape
    return values.reshape(extent_x // 2, 2, extent_y // 2, 2).sum(axis=(1, 3))


def prolong(values):
    return jnp.repeat(jnp.repeat(values, 2, axis=0), 2, axis=1)


def vcycle(source, hierarchy, padder, coarse_solve):
    if len(hierarchy) == 1:
        return coarse_solve(source, hierarchy[0])
    coeffs = hierarchy[0]
    iterate = relax_factor * source / coeffs[0]
    residue = source - level_apply(iterate, coeffs, padder)
    correction = vcycle(restrict(residue), hierarchy[1:], padder, coarse_solve)
    iterate = iterate + prolong(correction)
    return jacobi_sweep(iterate, source, coeffs, padder)


def block_inverse(matrix):
    extent = matrix.shape[0]
    identity = jnp.eye(extent, dtype=matrix.dtype)[:, :, None, None] * jnp.ones_like(matrix[0, 0])
    left_part, right_part = (matrix, identity)
    for pivot_row in range(extent):
        pivot_value = left_part[pivot_row, pivot_row]
        scaled_left = left_part[pivot_row] / pivot_value
        scaled_right = right_part[pivot_row] / pivot_value
        factor = left_part[:, pivot_row]
        left_part = left_part - factor[:, None] * scaled_left[None]
        right_part = right_part - factor[:, None] * scaled_right[None]
        left_part = left_part.at[pivot_row].set(scaled_left)
        right_part = right_part.at[pivot_row].set(scaled_right)
    return right_part


def pressure_coeffs(eff_diag, weights, face_trans, ghosts):

    def weighed(side_values):
        return jnp.sum(weights * side_values, axis=0)

    center = jnp.sum(weights * eff_diag[:, 0], axis=0)
    return jnp.stack(
        [
            center,
            -face_trans[0] * weighed(ghosts[0]),
            -face_trans[1] * weighed(ghosts[1]),
            -face_trans[2] * weighed(ghosts[2]),
            -face_trans[3] * weighed(ghosts[3]),
        ]
    )


def least_squares(start_norm, columns):
    steps_count = len(columns)
    rhs_list = [start_norm] + [jnp.zeros_like(start_norm)] * steps_count
    cosine_values, sine_values, upper_columns = ([], [], [])
    for column_no in range(steps_count):
        column = list(columns[column_no])
        for earlier in range(column_no):
            first_entry = column[earlier]
            second_entry = column[earlier + 1]
            column[earlier] = (
                cosine_values[earlier] * first_entry + sine_values[earlier] * second_entry
            )
            column[earlier + 1] = (
                -sine_values[earlier] * first_entry + cosine_values[earlier] * second_entry
            )
        radius = jnp.sqrt(
            column[column_no] * column[column_no] + column[column_no + 1] * column[column_no + 1]
        )
        cosine_value = column[column_no] / radius
        sine_value = column[column_no + 1] / radius
        column[column_no] = radius
        rhs_list[column_no + 1] = -sine_value * rhs_list[column_no]
        rhs_list[column_no] = cosine_value * rhs_list[column_no]
        cosine_values.append(cosine_value)
        sine_values.append(sine_value)
        upper_columns.append(column)
    coefficients = [None] * steps_count
    for row_no in reversed(range(steps_count)):
        running = rhs_list[row_no]
        for later_no in range(row_no + 1, steps_count):
            running = running - upper_columns[later_no][row_no] * coefficients[later_no]
        coefficients[row_no] = running / upper_columns[row_no][row_no]
    return (coefficients, jnp.abs(rhs_list[steps_count]))


def on_device(
    right_side, diag_blocks, couple_blocks, transmissibility, pressure_weights, well_mask
):
    identity = jnp.eye(NC, dtype=diag_blocks.dtype)[:, :, None, None]
    eff_diag = diag_blocks + well_boost * well_mask.astype(diag_blocks.dtype)[None, None] * identity
    inverse = block_inverse(eff_diag)
    ghost_padded = padded_2(couple_blocks[:, 0], (("gx", 1), ("gy", 2)), 1)
    ghosts = four_sides(ghost_padded)
    hierarchy = [pressure_coeffs(eff_diag, pressure_weights, transmissibility, ghosts)]
    for level_no in range(LEVELS - 1):
        hierarchy.append(coarsen(hierarchy[-1]))

    def coarse_solve(source, coeffs):
        return coarse_sweeps(source, coeffs, level_padder)

    def apply_full(vector):
        return apply_blocks(vector, eff_diag, couple_blocks, transmissibility, block_padder)

    start_norm = jnp.sqrt(lax.psum(jnp.sum(right_side * right_side), ("gx", "gy")))
    krylov_basis = [right_side / start_norm]
    directions, columns = ([], [])
    for step_no in range(GSTEPS):
        precondition_vector = krylov_basis[step_no]
        pressure_rhs = jnp.sum(pressure_weights * precondition_vector, axis=0)
        pressure = vcycle(pressure_rhs, hierarchy, level_padder, coarse_solve)
        lifted = jnp.concatenate(
            [pressure[None], jnp.zeros((NC - 1,) + pressure.shape, pressure.dtype)]
        )
        applied = apply_full(lifted)
        second = precondition_vector - applied
        direction = lifted + jnp.sum(inverse * second[None], axis=1)
        directions.append(direction)
        mapped = apply_full(direction)
        local_dots = jnp.stack(
            [jnp.sum(mapped * member) for member in krylov_basis] + [jnp.sum(mapped * mapped)]
        )
        summed = lax.psum(local_dots, ("gx", "gy"))
        projections = [summed[member_no] for member_no in range(len(krylov_basis))]
        squared = summed[len(krylov_basis)]
        remainder = mapped
        for projection, member in zip(projections, krylov_basis):
            remainder = remainder - projection * member
            squared = squared - projection * projection
        length = jnp.sqrt(squared)
        krylov_basis.append(remainder / length)
        columns.append(projections + [length])
    coefficients, estimate = least_squares(start_norm, columns)
    solution = coefficients[0] * directions[0]
    step_no = 1
    solution = solution + coefficients[step_no] * directions[step_no]
    return (solution, estimate)


def solution(mesh):
    return jax.shard_map(
        on_device,
        mesh=mesh,
        in_specs=(
            P(None, "gx", "gy"),
            P(None, None, "gx", "gy"),
            P(None, None, "gx", "gy"),
            P(None, "gx", "gy"),
            P(None, "gx", "gy"),
            P("gx", "gy"),
        ),
        out_specs=(P(None, "gx", "gy"), P()),
        check_vma=False,
    )
```

profile of v0, /device:TPU:0, one launch (start us, length us, event | category | flops | bytes accessed | tf_op | source)
XLA Modules:
  0.0 550.1 jit_solution(17748151497104485397)
XLA Ops:
  1.6 4.9 collective-permute-start.2
  15.5 44.7 %psum.21 = f32[]{:T(128)} all-reduce(f32[]{:T(128)} %multiply_reduce_fusion.18), channel_id=1, replica_groups=mesh['gx'=4,'gy'=8] {'gx','gy'}, use_global_device_ids=true, to_apply=%region_1.0 | all-reduce | flops 1 | bytes 8 | tf_op jit(solution)/shard_map/psum | solution.py:209
  97.3 4.5 collective-permute-start.9
  113.8 4.9 collective-permute-start.13
  140.5 4.5 collective-permute-start.19
  155.9 4.5 collective-permute-start.23
  171.3 4.5 collective-permute-start.27
  186.6 4.5 collective-permute-start.31
  202.1 4.5 collective-permute-start.35
  217.7 4.5 collective-permute-start.39
  239.5 4.6 collective-permute-start.43
  256.1 6.0 %collective-permute-start.47 = (f32[9,34,1]{2,1,0:T(8,128)S(1)}, f32[9,34,1]{2,1,0:T(8,128)S(1)}, u32[]{:S(2)}, u32[]{:S(2)}) collective-permute-start(f32[9,34,1]{2,1,0:T(8,128)S(1)} %get-tuple-element.263), channel_id=1, source_target_pairs={{0,1},{1,2},{2,3},{3,4},{4,5},{5,6},{6,7},{8,9},{9,10},{10,11},{11... | collective-permute-start | bytes 3680 | tf_op jit(solution)/shard_map/ppermute | solution.py:23
  266.1 45.3 %psum.22 = f32[2]{0:T(128)S(1)} all-reduce(f32[2]{0:T(128)S(1)} %pad_maximum_fusion.207), channel_id=1, replica_groups=mesh['gx'=4,'gy'=8] {'gx','gy'}, use_global_device_ids=true, to_apply=%region_35.0 | all-reduce | flops 2 | bytes 16 | tf_op jit(solution)/shard_map/psum | solution.py:227
  334.4 4.3 collective-permute-start.53
  373.4 4.5 collective-permute-start.63
  388.8 4.5 collective-permute-start.67
  404.1 4.5 collective-permute-start.71
  419.5 4.5 collective-permute-start.75
  435.0 4.5 collective-permute-start.79
  451.3 4.5 collective-permute-start.83
  468.2 4.6 collective-permute-start.87
  479.9 4.2 collective-permute-done.88
  485.6 6.0 %collective-permute-start.91 = (f32[9,34,1]{2,1,0:T(8,128)S(1)}, f32[9,34,1]{2,1,0:T(8,128)S(1)}, u32[]{:S(2)}, u32[]{:S(2)}) collective-permute-start(f32[9,34,1]{2,1,0:T(8,128)S(1)} %get-tuple-element.259), channel_id=1, source_target_pairs={{0,1},{1,2},{2,3},{3,4},{4,5},{5,6},{6,7},{8,9},{9,10},{10,11},{11... | collective-permute-start | bytes 3680 | tf_op jit(solution)/shard_map/ppermute | solution.py:23
  496.4 45.3 %psum.23 = f32[3]{0:T(128)S(1)} all-reduce(f32[3]{0:T(128)S(1)} %pad_maximum_fusion.208), channel_id=1, replica_groups=mesh['gx'=4,'gy'=8] {'gx','gy'}, use_global_device_ids=true, to_apply=%region_47.0 | all-reduce | flops 3 | bytes 24 | tf_op jit(solution)/shard_map/psum | solution.py:227
  (453 shorter events, 303.1 us)
Async XLA Ops:
  1.6 10.2 %collective-permute-start.2 = (f32[9,1,128]{2,1,0:T(1,128)S(1)}, f32[9,1,128]{2,1,0:T(1,128)S(1)}, u32[]{:S(2)}, u32[]{:S(2)}) collective-permute-start(f32[9,1,128]{2,1,0:T(1,128)S(1)} %get-tuple-element.277), channel_id=1, source_target_pairs={{0,8},{8,16},{16,24},{1,9},{9,17},{17,25},{2,10},{10,18},{18,26},{... | collective-permute-start | bytes 13832 | tf_op jit(solution)/shard_map/ppermute | solution.py:23
  12.8 54.1 %collective-permute-start.6 = (f32[9,34,1]{2,1,0:T(8,128)}, f32[9,34,1]{2,1,0:T(8,128)S(1)}, u32[]{:S(2)}, u32[]{:S(2)}) collective-permute-start(f32[9,34,1]{2,1,0:T(8,128)} %get-tuple-element.266), channel_id=1, source_target_pairs={{0,1},{1,2},{2,3},{3,4},{4,5},{5,6},{6,7},{8,9},{9,10},{10,11},{11... | collective-permute-start | bytes 3680 | tf_op jit(solution)/shard_map/ppermute | solution.py:23
  14.1 52.8 %collective-permute-start.4 = (f32[9,34,1]{2,1,0:T(8,128)S(1)}, f32[9,34,1]{2,1,0:T(8,128)S(1)}, u32[]{:S(2)}, u32[]{:S(2)}) collective-permute-start(f32[9,34,1]{2,1,0:T(8,128)S(1)} %get-tuple-element.267), channel_id=1, source_target_pairs={{1,0},{2,1},{3,2},{4,3},{5,4},{6,5},{7,6},{9,8},{10,9},{11,10},{12... | collective-permute-start | bytes 3680 | tf_op jit(solution)/shard_map/ppermute | solution.py:24
  68.1 22.1 %collective-permute-start.3 = (f32[1,128]{1,0:T(1,128)S(1)}, f32[1,128]{1,0:T(1,128)S(1)}, u32[]{:S(2)}, u32[]{:S(2)}) collective-permute-start(f32[1,128]{1,0:T(1,128)S(1)} %get-tuple-element.315), channel_id=1, source_target_pairs={{0,8},{8,16},{16,24},{1,9},{9,17},{17,25},{2,10},{10,18},{18,26},{... | collective-permute-start | bytes 1544 | tf_op jit(solution)/shard_map/ppermute | solution.py:23
  72.3 17.9 %collective-permute-start.1 = (f32[1,128]{1,0:T(1,128)S(1)}, f32[1,128]{1,0:T(1,128)S(1)}, u32[]{:S(2)}, u32[]{:S(2)}) collective-permute-start(f32[1,128]{1,0:T(1,128)S(1)} %get-tuple-element.316), channel_id=1, source_target_pairs={{8,0},{16,8},{24,16},{9,1},{17,9},{25,17},{10,2},{18,10},{26,18},{... | collective-permute-start | bytes 1544 | tf_op jit(solution)/shard_map/ppermute | solution.py:24
  97.3 6.6 %collective-permute-start.9 = (f32[1,64]{1,0:T(1,128)S(1)}, f32[1,64]{1,0:T(1,128)S(1)}, u32[]{:S(2)}, u32[]{:S(2)}) collective-permute-start(f32[1,64]{1,0:T(1,128)S(1)} %get-tuple-element.381), channel_id=1, source_target_pairs={{0,8},{8,16},{16,24},{1,9},{9,17},{17,25},{2,10},{10,18},{18,26},{... | collective-permute-start | bytes 776 | tf_op jit(solution)/shard_map/ppermute | solution.py:23
  101.9 6.2 %collective-permute-start.8 = (f32[1,64]{1,0:T(1,128)S(1)}, f32[1,64]{1,0:T(1,128)S(1)}, u32[]{:S(2)}, u32[]{:S(2)}) collective-permute-start(f32[1,64]{1,0:T(1,128)S(1)} %get-tuple-element.382), channel_id=1, source_target_pairs={{8,0},{16,8},{24,16},{9,1},{17,9},{25,17},{10,2},{18,10},{26,18},{... | collective-permute-start | bytes 776 | tf_op jit(solution)/shard_map/ppermute | solution.py:24
  113.8 6.3 %collective-permute-start.13 = (f32[1,32]{1,0:T(1,128)S(1)}, f32[1,32]{1,0:T(1,128)S(1)}, u32[]{:S(2)}, u32[]{:S(2)}) collective-permute-start(f32[1,32]{1,0:T(1,128)S(1)} %get-tuple-element.401), channel_id=1, source_target_pairs={{0,8},{8,16},{16,24},{1,9},{9,17},{17,25},{2,10},{10,18},{18,26},{... | collective-permute-start | bytes 392 | tf_op jit(solution)/shard_map/ppermute | solution.py:23
  139.3 5.8 %collective-permute-start.18 = (f32[10,1]{1,0:T(8,128)S(1)}, f32[10,1]{1,0:T(8,128)S(1)}, u32[]{:S(2)}, u32[]{:S(2)}) collective-permute-start(f32[10,1]{1,0:T(8,128)S(1)} %get-tuple-element.377), channel_id=1, source_target_pairs={{1,0},{2,1},{3,2},{4,3},{5,4},{6,5},{7,6},{9,8},{10,9},{11,10},{12... | collective-permute-start | bytes 128 | tf_op jit(solution)/shard_map/ppermute | solution.py:24
  154.6 5.8 %collective-permute-start.22 = (f32[10,1]{1,0:T(8,128)S(1)}, f32[10,1]{1,0:T(8,128)S(1)}, u32[]{:S(2)}, u32[]{:S(2)}) collective-permute-start(f32[10,1]{1,0:T(8,128)S(1)} %get-tuple-element.375), channel_id=1, source_target_pairs={{1,0},{2,1},{3,2},{4,3},{5,4},{6,5},{7,6},{9,8},{10,9},{11,10},{12... | collective-permute-start | bytes 128 | tf_op jit(solution)/shard_map/ppermute | solution.py:24
  170.0 5.8 %collective-permute-start.26 = (f32[10,1]{1,0:T(8,128)S(1)}, f32[10,1]{1,0:T(8,128)S(1)}, u32[]{:S(2)}, u32[]{:S(2)}) collective-permute-start(f32[10,1]{1,0:T(8,128)S(1)} %get-tuple-element.373), channel_id=1, source_target_pairs={{1,0},{2,1},{3,2},{4,3},{5,4},{6,5},{7,6},{9,8},{10,9},{11,10},{12... | collective-permute-start | bytes 128 | tf_op jit(solution)/shard_map/ppermute | solution.py:24
  185.3 5.8 %collective-permute-start.30 = (f32[10,1]{1,0:T(8,128)S(1)}, f32[10,1]{1,0:T(8,128)S(1)}, u32[]{:S(2)}, u32[]{:S(2)}) collective-permute-start(f32[10,1]{1,0:T(8,128)S(1)} %get-tuple-element.371), channel_id=1, source_target_pairs={{1,0},{2,1},{3,2},{4,3},{5,4},{6,5},{7,6},{9,8},{10,9},{11,10},{12... | collective-permute-start | bytes 128 | tf_op jit(solution)/shard_map/ppermute | solution.py:24
  200.9 5.8 %collective-permute-start.34 = (f32[18,1]{1,0:T(8,128)S(1)}, f32[18,1]{1,0:T(8,128)S(1)}, u32[]{:S(2)}, u32[]{:S(2)}) collective-permute-start(f32[18,1]{1,0:T(8,128)S(1)} %get-tuple-element.351), channel_id=1, source_target_pairs={{1,0},{2,1},{3,2},{4,3},{5,4},{6,5},{7,6},{9,8},{10,9},{11,10},{12... | collective-permute-start | bytes 224 | tf_op jit(solution)/shard_map/ppermute | solution.py:24
  216.4 5.9 %collective-permute-start.38 = (f32[34,1]{1,0:T(8,128)S(1)}, f32[34,1]{1,0:T(8,128)S(1)}, u32[]{:S(2)}, u32[]{:S(2)}) collective-permute-start(f32[34,1]{1,0:T(8,128)S(1)} %get-tuple-element.305), channel_id=1, source_target_pairs={{1,0},{2,1},{3,2},{4,3},{5,4},{6,5},{7,6},{9,8},{10,9},{11,10},{12... | collective-permute-start | bytes 416 | tf_op jit(solution)/shard_map/ppermute | solution.py:24
  238.2 6.0 %collective-permute-start.42 = (f32[9,34,1]{2,1,0:T(8,128)S(1)}, f32[9,34,1]{2,1,0:T(8,128)S(1)}, u32[]{:S(2)}, u32[]{:S(2)}) collective-permute-start(f32[9,34,1]{2,1,0:T(8,128)S(1)} %get-tuple-element.264), channel_id=1, source_target_pairs={{1,0},{2,1},{3,2},{4,3},{5,4},{6,5},{7,6},{9,8},{10,9},{11,10},{12... | collective-permute-start | bytes 3680 | tf_op jit(solution)/shard_map/ppermute | solution.py:24
  254.8 7.3 %collective-permute-start.46 = (f32[9,34,1]{2,1,0:T(8,128)S(1)}, f32[9,34,1]{2,1,0:T(8,128)S(1)}, u32[]{:S(2)}, u32[]{:S(2)}) collective-permute-start(f32[9,34,1]{2,1,0:T(8,128)S(1)} %get-tuple-element.262), channel_id=1, source_target_pairs={{1,0},{2,1},{3,2},{4,3},{5,4},{6,5},{7,6},{9,8},{10,9},{11,10},{12... | collective-permute-start | bytes 3680 | tf_op jit(solution)/shard_map/ppermute | solution.py:24
  256.1 7.0 %collective-permute-start.47 = (f32[9,34,1]{2,1,0:T(8,128)S(1)}, f32[9,34,1]{2,1,0:T(8,128)S(1)}, u32[]{:S(2)}, u32[]{:S(2)}) collective-permute-start(f32[9,34,1]{2,1,0:T(8,128)S(1)} %get-tuple-element.263), channel_id=1, source_target_pairs={{0,1},{1,2},{2,3},{3,4},{4,5},{5,6},{6,7},{8,9},{9,10},{10,11},{11... | collective-permute-start | bytes 3680 | tf_op jit(solution)/shard_map/ppermute | solution.py:23
  372.1 5.8 %collective-permute-start.62 = (f32[10,1]{1,0:T(8,128)S(1)}, f32[10,1]{1,0:T(8,128)S(1)}, u32[]{:S(2)}, u32[]{:S(2)}) collective-permute-start(f32[10,1]{1,0:T(8,128)S(1)} %get-tuple-element.363), channel_id=1, source_target_pairs={{1,0},{2,1},{3,2},{4,3},{5,4},{6,5},{7,6},{9,8},{10,9},{11,10},{12... | collective-permute-start | bytes 128 | tf_op jit(solution)/shard_map/ppermute | solution.py:24
  402.8 5.8 %collective-permute-start.70 = (f32[10,1]{1,0:T(8,128)S(1)}, f32[10,1]{1,0:T(8,128)S(1)}, u32[]{:S(2)}, u32[]{:S(2)}) collective-permute-start(f32[10,1]{1,0:T(8,128)S(1)} %get-tuple-element.359), channel_id=1, source_target_pairs={{1,0},{2,1},{3,2},{4,3},{5,4},{6,5},{7,6},{9,8},{10,9},{11,10},{12... | collective-permute-start | bytes 128 | tf_op jit(solution)/shard_map/ppermute | solution.py:24
  433.7 5.8 %collective-permute-start.78 = (f32[18,1]{1,0:T(8,128)S(1)}, f32[18,1]{1,0:T(8,128)S(1)}, u32[]{:S(2)}, u32[]{:S(2)}) collective-permute-start(f32[18,1]{1,0:T(8,128)S(1)} %get-tuple-element.347), channel_id=1, source_target_pairs={{1,0},{2,1},{3,2},{4,3},{5,4},{6,5},{7,6},{9,8},{10,9},{11,10},{12... | collective-permute-start | bytes 224 | tf_op jit(solution)/shard_map/ppermute | solution.py:24
  450.0 5.8 %collective-permute-start.82 = (f32[34,1]{1,0:T(8,128)S(1)}, f32[34,1]{1,0:T(8,128)S(1)}, u32[]{:S(2)}, u32[]{:S(2)}) collective-permute-start(f32[34,1]{1,0:T(8,128)S(1)} %get-tuple-element.301), channel_id=1, source_target_pairs={{1,0},{2,1},{3,2},{4,3},{5,4},{6,5},{7,6},{9,8},{10,9},{11,10},{12... | collective-permute-start | bytes 416 | tf_op jit(solution)/shard_map/ppermute | solution.py:24
  466.9 5.9 %collective-permute-start.86 = (f32[9,34,1]{2,1,0:T(8,128)S(1)}, f32[9,34,1]{2,1,0:T(8,128)S(1)}, u32[]{:S(2)}, u32[]{:S(2)}) collective-permute-start(f32[9,34,1]{2,1,0:T(8,128)S(1)} %get-tuple-element.260), channel_id=1, source_target_pairs={{1,0},{2,1},{3,2},{4,3},{5,4},{6,5},{7,6},{9,8},{10,9},{11,10},{12... | collective-permute-start | bytes 3680 | tf_op jit(solution)/shard_map/ppermute | solution.py:24
  484.3 8.1 %collective-permute-start.90 = (f32[9,34,1]{2,1,0:T(8,128)S(1)}, f32[9,34,1]{2,1,0:T(8,128)S(1)}, u32[]{:S(2)}, u32[]{:S(2)}) collective-permute-start(f32[9,34,1]{2,1,0:T(8,128)S(1)} %get-tuple-element.258), channel_id=1, source_target_pairs={{1,0},{2,1},{3,2},{4,3},{5,4},{6,5},{7,6},{9,8},{10,9},{11,10},{12... | collective-permute-start | bytes 3680 | tf_op jit(solution)/shard_map/ppermute | solution.py:24
  485.6 7.0 %collective-permute-start.91 = (f32[9,34,1]{2,1,0:T(8,128)S(1)}, f32[9,34,1]{2,1,0:T(8,128)S(1)}, u32[]{:S(2)}, u32[]{:S(2)}) collective-permute-start(f32[9,34,1]{2,1,0:T(8,128)S(1)} %get-tuple-element.259), channel_id=1, source_target_pairs={{0,1},{1,2},{2,3},{3,4},{4,5},{5,6},{6,7},{8,9},{9,10},{10,11},{11... | collective-permute-start | bytes 3680 | tf_op jit(solution)/shard_map/ppermute | solution.py:23
  (103 other events, 3451.6 us)
where the time goes:
time: 554 us; the launch traced here: 550 us
  starting transfers between devices  235 us (42%)
  blocking collectives  135 us (24%)
  waiting for transfers between devices  102 us (18%)
  other arithmetic  35.9 us (6%)
  local copies, waits for them, and re-layouts  28.1 us (5%)
  between operations  13.5 us (2%)
    ppermute x46, starting transfers between devices, padded_2(): before = lax.ppermute(last, axis, up)  176 us
    psum x2, blocking collectives, on_device(): summed = lax.psum(local_dots, ('gx', 'gy'))  90.7 us
    ppermute x46, waiting for transfers between devices, padded_2(): after = lax.ppermute(initial, axis, down)  84.8 us
    ppermute x46, starting transfers between devices, padded_2(): after = lax.ppermute(initial, axis, down)  59.4 us
    psum x1, blocking collectives, on_device(): lax.psum(jnp.sum(right_side * right_side), ('gx', 'gy'))  44.7 us
    ppermute x46, waiting for transfers between devices, padded_2(): before = lax.ppermute(last, axis, up)  17.3 us
  transfers between devices with their start and end apart: 92, of which 44 were waited for; matrix products, arithmetic and copies ran while one was open for 5% of the time, Pallas kernels for 0%

commit v1 on v0

v1 whole, which is shorter than its diff:
```python
import functools

import jax
import jax.numpy as jnp
from jax import lax
from jax.experimental import pallas as pl
from jax.experimental.pallas import tpu as pltpu
from jax.sharding import PartitionSpec as P

COARSE_SWEEPS = 6
RELAX = 0.8
KEEP = 1.0 - RELAX
BOOST = 8.0
MESH = pl.DeviceIdType.MESH
PIECE = 32
SIDES = ((-1, 0), (1, 0), (0, -1), (0, 1))
CORNERS = ((-1, -1), (-1, 1), (1, -1), (1, 1))


def roll(x, shift, axis):
    shift = shift % x.shape[axis]
    return x if shift == 0 else pltpu.roll(x, shift, axis)


def kernel(gx, gy, b_hbm, diag_hbm, couple_hbm, trans_hbm, weights_hbm, well_hbm, out_hbm, est_ref,
           vb, vd, vc, vt, vw, vwell, inv, coup, prod, z1, w1, q1, srow, rrow, scol, rcol,
           sown, spack, rx, ry, rd, sf, rfx, rfy, rfd, ext, link0, scaled0, link1, scaled1,
           scaled2, recip, fext, vout, sred, redy, sredx, redx,
           in_sem, ssem, rsem, ysend, yrecv, xsend, xrecv):
    nc, rows, cols = vb.shape
    ix, iy = lax.axis_index("gx"), lax.axis_index("gy")
    has = {(-1, 0): ix > 0, (1, 0): ix < gx - 1, (0, -1): iy > 0, (0, 1): iy < gy - 1}
    for dx, dy in CORNERS:
        has[(dx, dy)] = jnp.logical_and(has[(dx, 0)], has[(0, dy)])

    loads = []
    for n, (src, dst) in enumerate((
        (couple_hbm.at[:, 0], vc.at[:, 0]),
        (weights_hbm, vw),
        (trans_hbm, vt),
        (b_hbm, vb),
        (well_hbm, vwell),
        (diag_hbm, vd),
        (couple_hbm.at[:, pl.ds(1, nc - 1)], vc.at[:, pl.ds(1, nc - 1)]),
    )):
        copy = pltpu.make_async_copy(src, dst, in_sem.at[n])
        copy.start()
        loads.append(copy)

    row = lax.broadcasted_iota(jnp.int32, (rows, cols), 0)
    lane = lax.broadcasted_iota(jnp.int32, (rows, cols), 1)
    zero = jnp.zeros((rows, cols), jnp.float32)
    ones = jnp.ones((rows, cols), jnp.float32)

    first_piece = jnp.where(lane < PIECE, 1.0, 0.0)
    for s in range(2):
        for i in range(6):
            rx[s, i] = ones if i == 0 else zero
        ry[s, 0] = first_piece
        ry[s, 1] = zero
        rfx[s] = zero
        rfy[s] = zero
        for r in range(3):
            rrow[r, s] = jnp.zeros(rrow.shape[2:], jnp.float32)
            rcol[r, s] = zero
    for s in range(4):
        rd[s, 0] = first_piece
        rd[s, 1] = zero
        rfd[s] = zero

    barrier = pltpu.get_barrier_semaphore()
    for d in range(1, gy):
        pl.semaphore_signal(barrier, inc=1, device_id=(ix, lax.rem(iy + d, gy)), device_id_type=MESH)
    for d in range(1, gx):
        pl.semaphore_signal(barrier, inc=1, device_id=(lax.rem(ix + d, gx), iy), device_id_type=MESH)
    for dx, dy in CORNERS:
        @pl.when(has[(dx, dy)])
        def _(dx=dx, dy=dy):
            pl.semaphore_signal(barrier, inc=1, device_id=(ix + dx, iy + dy), device_id_type=MESH)
    near_x = has[(-1, 0)].astype(jnp.int32) + has[(1, 0)].astype(jnp.int32)
    near_y = has[(0, -1)].astype(jnp.int32) + has[(0, 1)].astype(jnp.int32)
    pl.semaphore_wait(barrier, gx + gy - 2 + near_x * near_y)

    sent = []

    def describe(k, src, dst, dx, dy):
        return pltpu.make_async_remote_copy(
            src_ref=src, dst_ref=dst, send_sem=ssem.at[k], recv_sem=rsem.at[k],
            device_id=(ix + dx, iy + dy), device_id_type=MESH)

    def send(k, src, dst, dx, dy):
        @pl.when(has[(dx, dy)])
        def _():
            describe(k, src, dst, dx, dy).start()
        sent.append((k, src, dst, dx, dy))

    def receive(group):
        for k, src, dst, dx, dy in group:
            @pl.when(has[(-dx, -dy)])
            def _(k=k, src=src, dst=dst, dx=dx, dy=dy):
                describe(k, src, dst, dx, dy).wait_recv()

    def send_edges(r, plane):
        low, high = zero, zero
        for c in range(nc):
            value = plane(c)
            srow[r, 0, c:c + 1] = value[0:1]
            srow[r, 1, c:c + 1] = value[rows - 1:rows]
            low = jnp.where(lane == c, roll(value, c, 1), low)
            high = jnp.where(lane == c, roll(value, c + 1, 1), high)
        scol[r, 0] = low
        scol[r, 1] = high
        mark = len(sent)
        send(4 * r, srow.at[r, 0], rrow.at[r, 1], -1, 0)
        send(4 * r + 1, srow.at[r, 1], rrow.at[r, 0], 1, 0)
        send(4 * r + 2, scol.at[r, 0], rcol.at[r, 1], 0, -1)
        send(4 * r + 3, scol.at[r, 1], rcol.at[r, 0], 0, 1)
        return sent[mark:]

    def neighbours(r, c, value):
        up = jnp.where(row == rows - 1, rrow[r, 1, c:c + 1], roll(value, -1, 0))
        down = jnp.where(row == 0, rrow[r, 0, c:c + 1], roll(value, 1, 0))
        north = jnp.where(lane == cols - 1, roll(rcol[r, 1], cols - 1 - c, 1), roll(value, -1, 1))
        south = jnp.where(lane == 0, roll(rcol[r, 0], -c, 1), roll(value, 1, 1))
        return up, down, north, south

    loads[0].wait()
    group = send_edges(0, lambda c: vc[c, 0])
    for copy in loads[1:6]:
        copy.wait()
    boost = BOOST * vwell[...].astype(jnp.float32)
    for c in range(nc):
        vd[c, c] = vd[c, c] + boost
    center = zero
    rhs = zero
    for c in range(nc):
        center = center + vw[c] * vd[c, 0]
        rhs = rhs + vw[c] * vb[c]
    sown[0] = center
    sown[5] = rhs
    receive(group)
    links = [zero] * 4
    for c in range(nc):
        for d, value in enumerate(neighbours(0, c, vc[c, 0])):
            value = vt[d] * value
            coup[d, c] = value
            links[d] = links[d] - vw[c] * value
    for d in range(4):
        sown[1 + d] = links[d]

    for side in range(2):
        for t in range(2):
            tile = zero
            for j in range(4):
                i = 4 * t + j
                if i < 6:
                    shift = PIECE * j + (PIECE if side else 0)
                    inside = jnp.logical_and(lane >= PIECE * j, lane < PIECE * (j + 1))
                    tile = jnp.where(inside, roll(sown[i], shift, 1), tile)
            spack[side, t] = tile
    mark = len(sent)
    for n, (dx, dy) in enumerate(SIDES):
        if dx:
            send(12 + n, sown, rx.at[(1 - dx) // 2], dx, dy)
        else:
            send(12 + n, spack.at[(1 + dy) // 2], ry.at[(1 - dy) // 2], dx, dy)
    for n, (dx, dy) in enumerate(CORNERS):
        send(16 + n, spack.at[(1 + dy) // 2], rd.at[3 - n], dx, dy)
    group = sent[mark:]

    def invert(step, carry):
        at = pl.ds(pl.multiple_of(step * 8, 8), 8)
        for i in range(nc):
            for j in range(nc):
                inv[i, j, at] = vd[i, j, at]
        for p in range(nc):
            reciprocal = 1.0 / inv[p, p, at]
            scaled = [reciprocal if j == p else inv[p, j, at] * reciprocal for j in range(nc)]
            for j in range(nc):
                inv[p, j, at] = scaled[j]
            for i in range(nc):
                if i != p:
                    factor = inv[i, p, at]
                    for j in range(nc):
                        if j == p:
                            inv[i, j, at] = -factor * scaled[j]
                        else:
                            inv[i, j, at] = inv[i, j, at] - factor * scaled[j]
        return carry

    lax.fori_loop(0, rows // 8, invert, 0)
    receive(group)

    for i in range(6):
        t, j = i // 4, i % 4
        fill = ones if i == 0 else zero
        for block in range(3):
            own = (rx[0, i], sown[i], rx[1, i])[block]
            left = (rd[0, t], ry[0, t], rd[2, t])[block]
            right = (rd[1, t], ry[1, t], rd[3, t])[block]
            right = roll(right, -PIECE * j, 1)
            left = roll(left, cols - PIECE - PIECE * j, 1)
            halo = jnp.where(lane < PIECE, right, jnp.where(lane >= cols - PIECE, left, fill))
            target = fext if i == 5 else ext.at[i]
            target[block * rows:(block + 1) * rows, 0:cols] = own
            target[block * rows:(block + 1) * rows, cols:2 * cols] = halo

    wide = (3 * rows, 2 * cols)
    wrow = lax.broadcasted_iota(jnp.int32, wide, 0)
    wlane = lax.broadcasted_iota(jnp.int32, wide, 1)

    def aggregate(x, s):
        x = x + jnp.where((wrow & s) == 0, roll(x, -s, 0), roll(x, s, 0))
        return x + jnp.where((wlane & s) == 0, roll(x, -s, 1), roll(x, s, 1))

    def around(x, s):
        return roll(x, -s, 0), roll(x, s, 0), roll(x, -s, 1), roll(x, s, 1)

    level = [ext[i] for i in range(5)]
    for k in range(3):
        ratio = RELAX / level[0]
        recip[k] = ratio
        for d in range(4):
            (scaled0, scaled1, scaled2)[k][d] = ratio * level[1 + d]
            if k < 2:
                (link0, link1)[k][d] = level[1 + d]
        if k < 2:
            s = 1 << k
            even_x, even_y = (wrow & s) == 0, (wlane & s) == 0
            c0, east, west, north, south = level
            level = [
                aggregate(c0 + jnp.where(even_x, east, west) + jnp.where(even_y, north, south), s),
                aggregate(jnp.where(even_x, 0.0, east), s),
                aggregate(jnp.where(even_x, west, 0.0), s),
                aggregate(jnp.where(even_y, 0.0, north), s),
                aggregate(jnp.where(even_y, south, 0.0), s),
            ]

    def gather_links(coeffs, x, s):
        total = None
        for d, value in enumerate(around(x, s)):
            term = coeffs[d] * value
            total = term if total is None else total + term
        return total

    def vcycle():
        f0 = fext[...]
        g0 = recip[0] * f0
        f1 = aggregate(KEEP * f0 - gather_links(link0, g0, 1), 1)
        g1 = recip[1] * f1
        f2 = aggregate(KEEP * f1 - gather_links(link1, g1, 2), 2)
        g2 = recip[2] * f2
        e2 = g2
        for _ in range(COARSE_SWEEPS - 1):
            e2 = KEEP * e2 + g2 - gather_links(scaled2, e2, 4)
        e1 = g1 + e2
        e1 = KEEP * e1 + g1 - gather_links(scaled1, e1, 2)
        e0 = g0 + e1
        fext[...] = KEEP * e0 + g0 - gather_links(scaled0, e0, 1)
        e0 = fext[...]
        return tuple(x[rows:2 * rows, 0:cols] for x in (e0,) + around(e0, 1))

    def precondition(source, target):
        p = vcycle()
        for c in range(nc):
            total = source[c] - vd[c, 0] * p[0]
            for d in range(4):
                total = total + coup[d, c] * p[1 + d]
            prod[c] = total
        for c in range(nc):
            total = p[0] if c == 0 else zero
            for k in range(nc):
                total = total + inv[c, k] * prod[k]
            target[c] = total

    def operate(r, source, target):
        for c in range(nc):
            total = vc[c, 0] * source[0]
            for k in range(1, nc):
                total = total + vc[c, k] * source[k]
            prod[c] = total
        group = send_edges(r, lambda c: prod[c])
        for c in range(nc):
            total = vd[c, 0] * source[0]
            for k in range(1, nc):
                total = total + vd[c, k] * source[k]
            target[c] = total
        receive(group)
        for c in range(nc):
            total = target[c]
            for d, value in enumerate(neighbours(r, c, prod[c])):
                total = total - vt[d] * value
            target[c] = total

    def dot(x, y):
        total = zero
        for c in range(nc):
            total = total + x(c) * y(c)
        return jnp.sum(total, axis=0, keepdims=True)

    def reduce_y(n, parts):
        sred[n] = jnp.zeros(sred.shape[1:], jnp.float32)
        for i, part in enumerate(parts):
            sred[n, i:i + 1] = part
        copies = []
        for d in range(1, gy):
            copy = pltpu.make_async_remote_copy(
                src_ref=sred.at[n], dst_ref=redy.at[n, iy], send_sem=ysend.at[n, d - 1],
                recv_sem=yrecv.at[n, d - 1], device_id=(ix, lax.rem(iy + d, gy)), device_id_type=MESH)
            copy.start()
            copies.append(copy)
        redy[n, iy] = sred[n]
        return copies

    def reduce_x(n, copies):
        for copy in copies:
            copy.wait()
        total = redy[n, 0]
        for i in range(1, gy):
            total = total + redy[n, i]
        sredx[n] = total
        copies = []
        for d in range(1, gx):
            copy = pltpu.make_async_remote_copy(
                src_ref=sredx.at[n], dst_ref=redx.at[n, ix], send_sem=xsend.at[n, d - 1],
                recv_sem=xrecv.at[n, d - 1], device_id=(lax.rem(ix + d, gx), iy), device_id_type=MESH)
            copy.start()
            copies.append(copy)
        redx[n, ix] = total
        return copies

    def reduced(n, copies):
        for copy in copies:
            copy.wait()
        total = redx[n, 0]
        for i in range(1, gx):
            total = total + redx[n, i]
        total = jnp.sum(total, axis=1, keepdims=True)
        return total[0:1], total[1:2], total[2:3]

    precondition(vb, z1)
    loads[6].wait()
    operate(1, z1, w1)

    rhs = zero
    for c in range(nc):
        rhs = rhs + vw[c] * w1[c]
    sf[...] = rhs
    mark = len(sent)
    for n, (dx, dy) in enumerate(SIDES):
        send(20 + n, sf, (rfx.at[(1 - dx) // 2] if dx else rfy.at[(1 - dy) // 2]), dx, dy)
    for n, (dx, dy) in enumerate(CORNERS):
        send(24 + n, sf, rfd.at[3 - n], dx, dy)
    group = sent[mark:]
    copies = reduce_y(0, [
        dot(lambda c: vb[c], lambda c: vb[c]),
        dot(lambda c: vb[c], lambda c: w1[c]),
        dot(lambda c: w1[c], lambda c: w1[c]),
    ])
    receive(group)
    for block in range(3):
        own = (rfx[0], sf[...], rfx[1])[block]
        left = (rfd[0], rfy[0], rfd[2])[block]
        right = (rfd[1], rfy[1], rfd[3])[block]
        fext[block * rows:(block + 1) * rows, 0:cols] = own
        fext[block * rows:(block + 1) * rows, cols:2 * cols] = jnp.where(lane < cols // 2, right, left)
    precondition(w1, q1)
    copies = reduce_x(0, copies)
    operate(2, q1, vout)

    bb, bw, ww = reduced(0, copies)
    beta = jnp.sqrt(bb)
    h11 = bw / bb
    h21 = jnp.sqrt(ww / bb - h11 * h11)
    scale = 1.0 / (beta * h21)
    over = 1.0 / beta

    def mapped(c):
        return (vout[c] - h11 * w1[c]) * scale

    def basis2(c):
        return (w1[c] - h11 * vb[c]) * scale

    copies = reduce_y(1, [
        dot(mapped, lambda c: vb[c] * over),
        dot(mapped, basis2),
        dot(mapped, mapped),
    ])
    h12, h22, squared = reduced(1, reduce_x(1, copies))
    h32 = jnp.sqrt(squared - h12 * h12 - h22 * h22)

    radius1 = jnp.sqrt(h11 * h11 + h21 * h21)
    cos1, sin1 = h11 / radius1, h21 / radius1
    top, low = cos1 * h12 + sin1 * h22, -sin1 * h12 + cos1 * h22
    radius2 = jnp.sqrt(low * low + h32 * h32)
    cos2, sin2 = low / radius2, h32 / radius2
    g0, g1 = cos1 * beta, -sin1 * beta
    g1, g2 = cos2 * g1, -sin2 * g1
    y2 = g1 / radius2
    y1 = (g0 - top * y2) / radius1
    est_ref[...] = jnp.abs(g2)
    second = y2 * scale
    first = y1 * over - second * h11
    for c in range(nc):
        out_hbm[c] = first * z1[c] + second * q1[c]

    for k, src, dst, dx, dy in sent:
        @pl.when(has[(dx, dy)])
        def _(k=k, src=src, dst=dst, dx=dx, dy=dy):
            describe(k, src, dst, dx, dy).wait_send()


def on_device(gx, gy, right_side, diag, couple, trans, weights, well):
    nc, rows, cols = right_side.shape
    f32 = jnp.float32
    wide = (3 * rows, 2 * cols)
    vm = lambda *shape: pltpu.VMEM(shape, f32)
    dma = lambda *shape: pltpu.SemaphoreType.DMA(shape)
    field = (nc, rows, cols)
    pad = -(-nc // 8) * 8
    out, est = pl.pallas_call(
        functools.partial(kernel, gx, gy),
        name="cpr_gmres",
        out_shape=(jax.ShapeDtypeStruct(field, f32), jax.ShapeDtypeStruct((1, 1), f32)),
        in_specs=[pl.BlockSpec(memory_space=pl.ANY)] * 6,
        out_specs=(pl.BlockSpec(memory_space=pltpu.VMEM), pl.BlockSpec(memory_space=pltpu.VMEM)),
        scratch_shapes=[
            vm(*field), vm(nc, *field), vm(nc, *field), vm(4, rows, cols), vm(*field),
            pltpu.VMEM((rows, cols), jnp.int32), vm(nc, *field), vm(4, *field),
            vm(*field), vm(*field), vm(*field), vm(*field),
            vm(3, 2, pad, cols), vm(3, 2, pad, cols), vm(3, 2, rows, cols), vm(3, 2, rows, cols),
            vm(6, rows, cols), vm(2, 2, rows, cols), vm(2, 6, rows, cols), vm(2, 2, rows, cols),
            vm(4, 2, rows, cols), vm(rows, cols), vm(2, rows, cols), vm(2, rows, cols),
            vm(4, rows, cols),
            vm(5, *wide), vm(4, *wide), vm(4, *wide), vm(4, *wide), vm(4, *wide),
            vm(4, *wide), vm(3, *wide), vm(*wide), vm(*field),
            vm(2, 8, cols), vm(2, gy, 8, cols), vm(2, 8, cols), vm(2, gx, 8, cols),
            dma(7), dma(28), dma(28), dma(2, gy - 1), dma(2, gy - 1), dma(2, gx - 1), dma(2, gx - 1),
        ],
        compiler_params=pltpu.CompilerParams(
            collective_id=0, has_side_effects=True, vmem_limit_bytes=48 << 20),
    )(right_side, diag, couple, trans, weights, well)
    return out, est.reshape(())


def solution(mesh):
    return jax.shard_map(
        functools.partial(on_device, mesh.shape["gx"], mesh.shape["gy"]),
        mesh=mesh,
        in_specs=(
            P(None, "gx", "gy"),
            P(None, None, "gx", "gy"),
            P(None, None, "gx", "gy"),
            P(None, "gx", "gy"),
            P(None, "gx", "gy"),
            P("gx", "gy"),
        ),
        out_specs=(P(None, "gx", "gy"), P()),
        check_vma=False,
    )
```

time: 554 us -> 49.5 us (0.09)
  starting transfers between devices: 235 us -> 0 us
  blocking collectives: 135 us -> 0 us
  waiting for transfers between devices: 102 us -> 0 us
  Pallas kernels: 0 us -> 40 us
  other arithmetic: 35.9 us -> 0 us
  local copies, waits for them, and re-layouts: 28.1 us -> 6.68 us
  between operations: 13.5 us -> 2.47 us
    ppermute x92 -> x0, starting transfers between devices: 235 us -> none  [the longest x46 176 us: padded_2(): before = lax.ppermute(last, axis, up)]
    psum x3 -> x0, blocking collectives: 135 us -> none  [the longest x2 90.7 us: on_device(): summed = lax.psum(local_dots, ('gx', 'gy'))]
    ppermute x92 -> x0, waiting for transfers between devices: 102 us -> none  [the longest x46 84.8 us: padded_2(): after = lax.ppermute(initial, axis, down)]
    pallas_call x0 -> x1, Pallas kernels: none -> 40 us  [on_device(): pl.pallas_call(functools.partial(kernel, gx, gy), name='cpr_gmres', out_s...]
    reduce_sum x23 -> x0, other arithmetic: 14.2 us -> none  [the longest x2 3.36 us: on_device(): jnp.sum(mapped * member)]
    reduce_sum x4 -> x0, local copies, waits for them, and re-layouts: 8 us -> none  [weighed(): return jnp.sum(weights * side_values, axis=0)]
    neg x4 -> x0, local copies, waits for them, and re-layouts: 6 us -> none  [the longest x1 2 us: pressure_coeffs(): -face_trans[2] * weighed(ghosts[2])]
    unnamed x70 -> x13, local copies, waits for them, and re-layouts: 0.89 us -> 6.68 us
  transfers between devices with their start and end apart: 92 -> 0, of which waited for: 44 -> 0; matrix products, arithmetic and copies ran while one was open for 5% -> 0% of each run, Pallas kernels for 0% -> 0%
where the time goes in v1:
time: 49.5 us; the launch traced here: 49.1 us
  Pallas kernels  40 us (81%)
  local copies, waits for them, and re-layouts  6.68 us (13%)
  between operations  2.47 us (5%)
    pallas_call x1, Pallas kernels, on_device(): pl.pallas_call(functools.partial(kernel, gx, gy), name='cpr_gmres', out_s...  40 us
    unnamed x13, local copies, waits for them, and re-layouts  6.68 us

profile of v1, /device:TPU:0, one launch (start us, length us, event | category | flops | bytes accessed | tf_op | source)
XLA Modules:
  0.0 49.1 jit_solution(17786754534673018172)
XLA Ops:
  0.6 0.0 copy-start
  0.6 1.3 %copy-done = f32[9,9,32,128]{3,2,1,0:T(8,128)S(1)} copy-done((f32[9,9,32,128]{3,2,1,0:T(8,128)S(1)}, f32[9,9,32,128]{3,2,1,0:T(8,128)}, u32[]{:S(2)}) %copy-start) | copy-done | bytes 1327128
  2.0 0.0 copy-start.1
  2.0 1.3 %copy-done.1 = f32[9,9,32,128]{3,2,1,0:T(8,128)S(1)} copy-done((f32[9,9,32,128]{3,2,1,0:T(8,128)S(1)}, f32[9,9,32,128]{3,2,1,0:T(8,128)}, u32[]{:S(2)}) %copy-start.1) | copy-done | bytes 1327128
  3.3 0.0 copy-start.2
  3.3 0.9 %copy-done.2 = f32[9,32,128]{2,1,0:T(8,128)S(1)} copy-done((f32[9,32,128]{2,1,0:T(8,128)S(1)}, f32[9,32,128]{2,1,0:T(8,128)}, u32[]{:S(2)}) %copy-start.2) | copy-done | bytes 147480
  4.2 0.0 copy-start.3
  4.2 0.9 %copy-done.3 = f32[9,32,128]{2,1,0:T(8,128)S(1)} copy-done((f32[9,32,128]{2,1,0:T(8,128)S(1)}, f32[9,32,128]{2,1,0:T(8,128)}, u32[]{:S(2)}) %copy-start.3) | copy-done | bytes 147480
  5.1 0.0 copy-start.4
  5.1 0.8 %copy-done.4 = f32[4,32,128]{2,1,0:T(8,128)S(1)} copy-done((f32[4,32,128]{2,1,0:T(8,128)S(1)}, f32[4,32,128]{2,1,0:T(8,128)}, u32[]{:S(2)}) %copy-start.4) | copy-done | bytes 65560
  5.9 0.0 copy-start.5
  5.9 0.7 %copy-done.5 = s32[32,128]{1,0:T(8,128)S(1)} copy-done((s32[32,128]{1,0:T(8,128)S(1)}, s32[32,128]{1,0:T(8,128)}, u32[]{:S(2)}) %copy-start.5) | copy-done | bytes 16408
  6.7 40.0 %cpr_gmres.1 = (f32[9,32,128]{2,1,0:T(8,128)S(1)}, f32[1,1]{1,0:T(1,128)}) custom-call(f32[9,32,128]{2,1,0:T(8,128)S(1)} %copy-done.2, f32[9,9,32,128]{3,2,1,0:T(8,128)S(1)} %copy-done, f32[9,9,32,128]{3,2,1,0:T(8,128)S(1)} %copy-done.1, f32[4,32,128]{2,1,0:T(8,128)S(1)} %copy-done.4, f32[9,32,128]{2,1,0:T(8,128)S(1)} %copy-done.3, s32[32,128]{1,0:T(8,128)S(1)} %copy-done.5), custom_call_target="tpu_custom_call" | custom-call | tf_op jit(solution)/shard_map/cpr_gmres/pallas_call | solution.py:421
  46.7 0.7 %copy.10 = f32[9,32,128]{2,1,0:T(8,128)} copy(f32[9,32,128]{2,1,0:T(8,128)S(1)} %get-tuple-element.8) | data formatting | bytes 294912
Async XLA Ops:
  0.6 1.3 %copy-start = (f32[9,9,32,128]{3,2,1,0:T(8,128)S(1)}, f32[9,9,32,128]{3,2,1,0:T(8,128)}, u32[]{:S(2)}) copy-start(f32[9,9,32,128]{3,2,1,0:T(8,128)} %diag_hbm.1) | copy-start | bytes 3981316
  2.0 1.3 %copy-start.1 = (f32[9,9,32,128]{3,2,1,0:T(8,128)S(1)}, f32[9,9,32,128]{3,2,1,0:T(8,128)}, u32[]{:S(2)}) copy-start(f32[9,9,32,128]{3,2,1,0:T(8,128)} %couple_hbm.1) | copy-start | bytes 3981316
  3.3 0.9 %copy-start.2 = (f32[9,32,128]{2,1,0:T(8,128)S(1)}, f32[9,32,128]{2,1,0:T(8,128)}, u32[]{:S(2)}) copy-start(f32[9,32,128]{2,1,0:T(8,128)} %b_hbm.1) | copy-start | bytes 442372
  4.2 0.9 %copy-start.3 = (f32[9,32,128]{2,1,0:T(8,128)S(1)}, f32[9,32,128]{2,1,0:T(8,128)}, u32[]{:S(2)}) copy-start(f32[9,32,128]{2,1,0:T(8,128)} %weights_hbm.1) | copy-start | bytes 442372
  5.1 0.8 %copy-start.4 = (f32[4,32,128]{2,1,0:T(8,128)S(1)}, f32[4,32,128]{2,1,0:T(8,128)}, u32[]{:S(2)}) copy-start(f32[4,32,128]{2,1,0:T(8,128)} %trans_hbm.1) | copy-start | bytes 196612
  5.9 0.7 %copy-start.5 = (s32[32,128]{1,0:T(8,128)S(1)}, s32[32,128]{1,0:T(8,128)}, u32[]{:S(2)}) copy-start(s32[32,128]{1,0:T(8,128)} %well_hbm.1) | copy-start | bytes 49156

commit v2 on v1

--- a/solution.py
+++ b/solution.py
@@ -422,7 +422,7 @@
         functools.partial(kernel, gx, gy),
         name="cpr_gmres",
         out_shape=(jax.ShapeDtypeStruct(field, f32), jax.ShapeDtypeStruct((1, 1), f32)),
-        in_specs=[pl.BlockSpec(memory_space=pl.ANY)] * 6,
+        in_specs=[pl.BlockSpec(memory_space=pltpu.HBM)] * 6,
         out_specs=(pl.BlockSpec(memory_space=pltpu.VMEM), pl.BlockSpec(memory_space=pltpu.VMEM)),
         scratch_shapes=[
             vm(*field), vm(nc, *field), vm(nc, *field), vm(4, rows, cols), vm(*field),
@@ -438,7 +438,7 @@
             dma(7), dma(28), dma(28), dma(2, gy - 1), dma(2, gy - 1), dma(2, gx - 1), dma(2, gx - 1),
         ],
         compiler_params=pltpu.CompilerParams(
-            collective_id=0, has_side_effects=True, vmem_limit_bytes=48 << 20),
+            collective_id=0, has_side_effects=True, vmem_limit_bytes=60 << 20),
     )(right_side, diag, couple, trans, weights, well)
     return out, est.reshape(())
 

time: 49.5 us -> 43.5 us (0.88)
  local copies, waits for them, and re-layouts: 6.68 us -> 1.58 us
  Pallas kernels: 40 us -> 39.4 us
    unnamed x13 -> x1, local copies, waits for them, and re-layouts: 6.68 us -> 1.58 us
    pallas_call x1, Pallas kernels: 40 us -> 39.4 us  [on_device(): pl.pallas_call(functools.partial(kernel, gx, gy), name='cpr_gmres', out_s...]
where the time goes in v2:
time: 43.5 us; the launch traced here: 43.4 us
  Pallas kernels  39.4 us (91%)
  between operations  2.39 us (5%)
  local copies, waits for them, and re-layouts  1.58 us (4%)
    pallas_call x1, Pallas kernels, on_device(): pl.pallas_call(functools.partial(kernel, gx, gy), name='cpr_gmres', out_s...  39.4 us
    unnamed x1, local copies, waits for them, and re-layouts  1.58 us

profile of v2, /device:TPU:0, one launch (start us, length us, event | category | flops | bytes accessed | tf_op | source)
XLA Modules:
  0.0 43.4 jit_solution(974358812036197066)
XLA Ops:
  0.6 39.4 %cpr_gmres.1 = (f32[9,32,128]{2,1,0:T(8,128)}, f32[1,1]{1,0:T(1,128)}) custom-call(f32[9,32,128]{2,1,0:T(8,128)} %b_hbm.1, f32[9,9,32,128]{3,2,1,0:T(8,128)} %diag_hbm.1, f32[9,9,32,128]{3,2,1,0:T(8,128)} %couple_hbm.1, f32[4,32,128]{2,1,0:T(8,128)} %trans_hbm.1, f32[9,32,128]{2,1,0:T(8,128)} %weights_hbm.1, s32[32,128]{1,0:T(8,128)} %well_hbm.1), custom_call_target="tpu_custom_call" | custom-call | tf_op jit(solution)/shard_map/cpr_gmres/pallas_call | solution.py:421
  40.0 1.6 %copy.10 = f32[9,32,128]{2,1,0:T(8,128)} copy(f32[9,32,128]{2,1,0:T(8,128)} %get-tuple-element.8) | data formatting | bytes 294912

commit v3 on v2

--- a/solution.py
+++ b/solution.py
@@ -24,9 +24,9 @@
 
 def kernel(gx, gy, b_hbm, diag_hbm, couple_hbm, trans_hbm, weights_hbm, well_hbm, out_hbm, est_ref,
            vb, vd, vc, vt, vw, vwell, inv, coup, prod, z1, w1, q1, srow, rrow, scol, rcol,
-           sown, spack, rx, ry, rd, sf, rfx, rfy, rfd, ext, link0, scaled0, link1, scaled1,
-           scaled2, recip, fext, vout, sred, redy, sredx, redx,
-           in_sem, ssem, rsem, ysend, yrecv, xsend, xrecv):
+           sown, spack, rx, ry, rd, sf, sfp, rfx, rfy, rfd, ext, link0, scaled0, link1, scaled1,
+           scaled2, recip, fext, vout, sred, redall,
+           in_sem, ssem, rsem, rsend, rrecv):
     nc, rows, cols = vb.shape
     ix, iy = lax.axis_index("gx"), lax.axis_index("gy")
     has = {(-1, 0): ix > 0, (1, 0): ix < gx - 1, (0, -1): iy > 0, (0, 1): iy < gy - 1}
@@ -40,7 +40,8 @@
         (trans_hbm, vt),
         (b_hbm, vb),
         (well_hbm, vwell),
-        (diag_hbm, vd),
+        (diag_hbm.at[:, 0], vd.at[:, 0]),
+        (diag_hbm.at[:, pl.ds(1, nc - 1)], vd.at[:, pl.ds(1, nc - 1)]),
         (couple_hbm.at[:, pl.ds(1, nc - 1)], vc.at[:, pl.ds(1, nc - 1)]),
     )):
         copy = pltpu.make_async_copy(src, dst, in_sem.at[n])
@@ -52,34 +53,52 @@
     zero = jnp.zeros((rows, cols), jnp.float32)
     ones = jnp.ones((rows, cols), jnp.float32)
 
-    first_piece = jnp.where(lane < PIECE, 1.0, 0.0)
+    blank = jnp.zeros((8, cols), jnp.float32)
     for s in range(2):
         for i in range(6):
             rx[s, i] = ones if i == 0 else zero
-        ry[s, 0] = first_piece
-        ry[s, 1] = zero
+            ry[s, i] = blank + 1.0 if i == 0 else blank
         rfx[s] = zero
-        rfy[s] = zero
+        rfy[s] = blank
         for r in range(3):
             rrow[r, s] = jnp.zeros(rrow.shape[2:], jnp.float32)
             rcol[r, s] = zero
     for s in range(4):
-        rd[s, 0] = first_piece
-        rd[s, 1] = zero
-        rfd[s] = zero
+        for i in range(6):
+            rd[s, i] = blank + 1.0 if i == 0 else blank
+        rfd[s] = blank
 
     barrier = pltpu.get_barrier_semaphore()
-    for d in range(1, gy):
-        pl.semaphore_signal(barrier, inc=1, device_id=(ix, lax.rem(iy + d, gy)), device_id_type=MESH)
-    for d in range(1, gx):
-        pl.semaphore_signal(barrier, inc=1, device_id=(lax.rem(ix + d, gx), iy), device_id_type=MESH)
-    for dx, dy in CORNERS:
-        @pl.when(has[(dx, dy)])
-        def _(dx=dx, dy=dy):
-            pl.semaphore_signal(barrier, inc=1, device_id=(ix + dx, iy + dy), device_id_type=MESH)
-    near_x = has[(-1, 0)].astype(jnp.int32) + has[(1, 0)].astype(jnp.int32)
-    near_y = has[(0, -1)].astype(jnp.int32) + has[(0, 1)].astype(jnp.int32)
-    pl.semaphore_wait(barrier, gx + gy - 2 + near_x * near_y)
+    count = gx * gy
+    me = ix * gy + iy
+
+    def greet(d, carry):
+        target = lax.rem(me + d, count)
+        pl.semaphore_signal(barrier, inc=1, device_id=(lax.div(target, gy), lax.rem(target, gy)),
+                            device_id_type=MESH)
+        return carry
+
+    lax.fori_loop(1, count, greet, 0)
+    pl.semaphore_wait(barrier, count - 1)
+
+    groups = rows // 8
+    tile_lane = lane[0:8]
+
+    def pack(plane, side):
+        tile = jnp.zeros((8, cols), jnp.float32)
+        for j in range(groups):
+            inside = jnp.logical_and(tile_lane >= PIECE * j, tile_lane < PIECE * (j + 1))
+            tile = jnp.where(inside, roll(plane[8 * j:8 * j + 8], PIECE * (j + side), 1), tile)
+        return tile
+
+    def unpack(left, right, fill):
+        parts = []
+        for j in range(groups):
+            first = roll(right, -PIECE * j, 1)
+            last = roll(left, -PIECE * (j + 1), 1)
+            parts.append(jnp.where(tile_lane < PIECE, first,
+                                   jnp.where(tile_lane >= cols - PIECE, last, fill)))
+        return jnp.concatenate(parts, axis=0)
 
     sent = []
 
@@ -129,8 +148,7 @@
     for copy in loads[1:6]:
         copy.wait()
     boost = BOOST * vwell[...].astype(jnp.float32)
-    for c in range(nc):
-        vd[c, c] = vd[c, c] + boost
+    vd[0, 0] = vd[0, 0] + boost
     center = zero
     rhs = zero
     for c in range(nc):
@@ -149,15 +167,8 @@
         sown[1 + d] = links[d]
 
     for side in range(2):
-        for t in range(2):
-            tile = zero
-            for j in range(4):
-                i = 4 * t + j
-                if i < 6:
-                    shift = PIECE * j + (PIECE if side else 0)
-                    inside = jnp.logical_and(lane >= PIECE * j, lane < PIECE * (j + 1))
-                    tile = jnp.where(inside, roll(sown[i], shift, 1), tile)
-            spack[side, t] = tile
+        for i in range(6):
+            spack[side, i] = pack(sown[i], side)
     mark = len(sent)
     for n, (dx, dy) in enumerate(SIDES):
         if dx:
@@ -167,6 +178,10 @@
     for n, (dx, dy) in enumerate(CORNERS):
         send(16 + n, spack.at[(1 + dy) // 2], rd.at[3 - n], dx, dy)
     group = sent[mark:]
+
+    loads[6].wait()
+    for c in range(1, nc):
+        vd[c, c] = vd[c, c] + boost
 
     def invert(step, carry):
         at = pl.ds(pl.multiple_of(step * 8, 8), 8)
@@ -192,15 +207,12 @@
     receive(group)
 
     for i in range(6):
-        t, j = i // 4, i % 4
-        fill = ones if i == 0 else zero
+        fill = 1.0 if i == 0 else 0.0
         for block in range(3):
             own = (rx[0, i], sown[i], rx[1, i])[block]
-            left = (rd[0, t], ry[0, t], rd[2, t])[block]
-            right = (rd[1, t], ry[1, t], rd[3, t])[block]
-            right = roll(right, -PIECE * j, 1)
-            left = roll(left, cols - PIECE - PIECE * j, 1)
-            halo = jnp.where(lane < PIECE, right, jnp.where(lane >= cols - PIECE, left, fill))
+            left = (rd[0, i], ry[0, i], rd[2, i])[block]
+            right = (rd[1, i], ry[1, i], rd[3, i])[block]
+            halo = unpack(left, right, fill)
             target = fext if i == 5 else ext.at[i]
             target[block * rows:(block + 1) * rows, 0:cols] = own
             target[block * rows:(block + 1) * rows, cols:2 * cols] = halo
@@ -298,61 +310,55 @@
             total = total + x(c) * y(c)
         return jnp.sum(total, axis=0, keepdims=True)
 
-    def reduce_y(n, parts):
+    def part_copy(n, d):
+        target = lax.rem(me + d, count)
+        return pltpu.make_async_remote_copy(
+            src_ref=sred.at[n], dst_ref=redall.at[n, me], send_sem=rsend.at[n, d - 1],
+            recv_sem=rrecv.at[n, d - 1], device_id=(lax.div(target, gy), lax.rem(target, gy)),
+            device_id_type=MESH)
+
+    def start_reduce(n, parts):
         sred[n] = jnp.zeros(sred.shape[1:], jnp.float32)
         for i, part in enumerate(parts):
             sred[n, i:i + 1] = part
-        copies = []
-        for d in range(1, gy):
-            copy = pltpu.make_async_remote_copy(
-                src_ref=sred.at[n], dst_ref=redy.at[n, iy], send_sem=ysend.at[n, d - 1],
-                recv_sem=yrecv.at[n, d - 1], device_id=(ix, lax.rem(iy + d, gy)), device_id_type=MESH)
-            copy.start()
-            copies.append(copy)
-        redy[n, iy] = sred[n]
-        return copies
-
-    def reduce_x(n, copies):
-        for copy in copies:
-            copy.wait()
-        total = redy[n, 0]
-        for i in range(1, gy):
-            total = total + redy[n, i]
-        sredx[n] = total
-        copies = []
-        for d in range(1, gx):
-            copy = pltpu.make_async_remote_copy(
-                src_ref=sredx.at[n], dst_ref=redx.at[n, ix], send_sem=xsend.at[n, d - 1],
-                recv_sem=xrecv.at[n, d - 1], device_id=(lax.rem(ix + d, gx), iy), device_id_type=MESH)
-            copy.start()
-            copies.append(copy)
-        redx[n, ix] = total
-        return copies
-
-    def reduced(n, copies):
-        for copy in copies:
-            copy.wait()
-        total = redx[n, 0]
-        for i in range(1, gx):
-            total = total + redx[n, i]
+
+        def start(d, carry):
+            part_copy(n, d).start()
+            return carry
+
+        lax.fori_loop(1, count, start, 0)
+        redall[n, me] = sred[n]
+
+    def reduced(n):
+        def finish(d, carry):
+            part_copy(n, d).wait()
+            return carry
+
+        lax.fori_loop(1, count, finish, 0)
+        total = lax.fori_loop(1, count, lambda i, t: t + redall[n, i], redall[n, 0])
         total = jnp.sum(total, axis=1, keepdims=True)
         return total[0:1], total[1:2], total[2:3]
 
     precondition(vb, z1)
-    loads[6].wait()
+    loads[7].wait()
     operate(1, z1, w1)
 
     rhs = zero
     for c in range(nc):
         rhs = rhs + vw[c] * w1[c]
     sf[...] = rhs
+    for side in range(2):
+        sfp[side] = pack(rhs, side)
     mark = len(sent)
     for n, (dx, dy) in enumerate(SIDES):
-        send(20 + n, sf, (rfx.at[(1 - dx) // 2] if dx else rfy.at[(1 - dy) // 2]), dx, dy)
+        if dx:
+            send(20 + n, sf, rfx.at[(1 - dx) // 2], dx, dy)
+        else:
+            send(20 + n, sfp.at[(1 + dy) // 2], rfy.at[(1 - dy) // 2], dx, dy)
     for n, (dx, dy) in enumerate(CORNERS):
-        send(24 + n, sf, rfd.at[3 - n], dx, dy)
+        send(24 + n, sfp.at[(1 + dy) // 2], rfd.at[3 - n], dx, dy)
     group = sent[mark:]
-    copies = reduce_y(0, [
+    start_reduce(0, [
         dot(lambda c: vb[c], lambda c: vb[c]),
         dot(lambda c: vb[c], lambda c: w1[c]),
         dot(lambda c: w1[c], lambda c: w1[c]),
@@ -363,12 +369,11 @@
         left = (rfd[0], rfy[0], rfd[2])[block]
         right = (rfd[1], rfy[1], rfd[3])[block]
         fext[block * rows:(block + 1) * rows, 0:cols] = own
-        fext[block * rows:(block + 1) * rows, cols:2 * cols] = jnp.where(lane < cols // 2, right, left)
+        fext[block * rows:(block + 1) * rows, cols:2 * cols] = unpack(left, right, 0.0)
     precondition(w1, q1)
-    copies = reduce_x(0, copies)
     operate(2, q1, vout)
 
-    bb, bw, ww = reduced(0, copies)
+    bb, bw, ww = reduced(0)
     beta = jnp.sqrt(bb)
     h11 = bw / bb
     h21 = jnp.sqrt(ww / bb - h11 * h11)
@@ -381,12 +386,12 @@
     def basis2(c):
         return (w1[c] - h11 * vb[c]) * scale
 
-    copies = reduce_y(1, [
+    start_reduce(1, [
         dot(mapped, lambda c: vb[c] * over),
         dot(mapped, basis2),
         dot(mapped, mapped),
     ])
-    h12, h22, squared = reduced(1, reduce_x(1, copies))
+    h12, h22, squared = reduced(1)
     h32 = jnp.sqrt(squared - h12 * h12 - h22 * h22)
 
     radius1 = jnp.sqrt(h11 * h11 + h21 * h21)
@@ -429,13 +434,13 @@
             pltpu.VMEM((rows, cols), jnp.int32), vm(nc, *field), vm(4, *field),
             vm(*field), vm(*field), vm(*field), vm(*field),
             vm(3, 2, pad, cols), vm(3, 2, pad, cols), vm(3, 2, rows, cols), vm(3, 2, rows, cols),
-            vm(6, rows, cols), vm(2, 2, rows, cols), vm(2, 6, rows, cols), vm(2, 2, rows, cols),
-            vm(4, 2, rows, cols), vm(rows, cols), vm(2, rows, cols), vm(2, rows, cols),
-            vm(4, rows, cols),
+            vm(6, rows, cols), vm(2, 6, 8, cols), vm(2, 6, rows, cols), vm(2, 6, 8, cols),
+            vm(4, 6, 8, cols), vm(rows, cols), vm(2, 8, cols), vm(2, rows, cols), vm(2, 8, cols),
+            vm(4, 8, cols),
             vm(5, *wide), vm(4, *wide), vm(4, *wide), vm(4, *wide), vm(4, *wide),
             vm(4, *wide), vm(3, *wide), vm(*wide), vm(*field),
-            vm(2, 8, cols), vm(2, gy, 8, cols), vm(2, 8, cols), vm(2, gx, 8, cols),
-            dma(7), dma(28), dma(28), dma(2, gy - 1), dma(2, gy - 1), dma(2, gx - 1), dma(2, gx - 1),
+            vm(2, 8, cols), vm(2, gx * gy, 8, cols),
+            dma(8), dma(28), dma(28), dma(2, gx * gy - 1), dma(2, gx * gy - 1),
         ],
         compiler_params=pltpu.CompilerParams(
             collective_id=0, has_side_effects=True, vmem_limit_bytes=60 << 20),

time: 43.5 us -> 43.1 us (level)
  no operation moved by 1% of the time
where the time goes in v3:
time: 43.1 us; the launch traced here: 42.9 us
  Pallas kernels  39 us (90%)
  between operations  2.39 us (6%)
  local copies, waits for them, and re-layouts  1.58 us (4%)
    pallas_call x1, Pallas kernels, on_device(): pl.pallas_call(functools.partial(kernel, gx, gy), name='cpr_gmres', out_s...  39 us
    unnamed x1, local copies, waits for them, and re-layouts  1.58 us

profile of v3, /device:TPU:0, one launch (start us, length us, event | category | flops | bytes accessed | tf_op | source)
XLA Modules:
  0.0 42.9 jit_solution(17139124405814680681)
XLA Ops:
  0.6 39.0 %cpr_gmres.1 = (f32[9,32,128]{2,1,0:T(8,128)}, f32[1,1]{1,0:T(1,128)}) custom-call(f32[9,32,128]{2,1,0:T(8,128)} %b_hbm.1, f32[9,9,32,128]{3,2,1,0:T(8,128)} %diag_hbm.1, f32[9,9,32,128]{3,2,1,0:T(8,128)} %couple_hbm.1, f32[4,32,128]{2,1,0:T(8,128)} %trans_hbm.1, f32[9,32,128]{2,1,0:T(8,128)} %weights_hbm.1, s32[32,128]{1,0:T(8,128)} %well_hbm.1), custom_call_target="tpu_custom_call" | custom-call | tf_op jit(solution)/shard_map/cpr_gmres/pallas_call | solution.py:426
  39.6 1.6 %copy.10 = f32[9,32,128]{2,1,0:T(8,128)} copy(f32[9,32,128]{2,1,0:T(8,128)} %get-tuple-element.8) | data formatting | bytes 294912

commit v4 on v3

--- a/solution.py
+++ b/solution.py
@@ -25,8 +25,8 @@
 def kernel(gx, gy, b_hbm, diag_hbm, couple_hbm, trans_hbm, weights_hbm, well_hbm, out_hbm, est_ref,
            vb, vd, vc, vt, vw, vwell, inv, coup, prod, z1, w1, q1, srow, rrow, scol, rcol,
            sown, spack, rx, ry, rd, sf, sfp, rfx, rfy, rfd, ext, link0, scaled0, link1, scaled1,
-           scaled2, recip, fext, vout, sred, redall,
-           in_sem, ssem, rsem, rsend, rrecv):
+           scaled2, recip, fext, vout, sred, redy, redx, redall,
+           in_sem, ssem, rsem, ysend, yrecv, xsend, xrecv, rsend, rrecv):
     nc, rows, cols = vb.shape
     ix, iy = lax.axis_index("gx"), lax.axis_index("gy")
     has = {(-1, 0): ix > 0, (1, 0): ix < gx - 1, (0, -1): iy > 0, (0, 1): iy < gy - 1}
@@ -72,14 +72,17 @@
     count = gx * gy
     me = ix * gy + iy
 
-    def greet(d, carry):
-        target = lax.rem(me + d, count)
-        pl.semaphore_signal(barrier, inc=1, device_id=(lax.div(target, gy), lax.rem(target, gy)),
-                            device_id_type=MESH)
-        return carry
-
-    lax.fori_loop(1, count, greet, 0)
-    pl.semaphore_wait(barrier, count - 1)
+    for d in range(1, gy):
+        pl.semaphore_signal(barrier, inc=1, device_id=(ix, lax.rem(iy + d, gy)), device_id_type=MESH)
+    for d in range(1, gx):
+        pl.semaphore_signal(barrier, inc=1, device_id=(lax.rem(ix + d, gx), iy), device_id_type=MESH)
+    for dx, dy in CORNERS:
+        @pl.when(has[(dx, dy)])
+        def _(dx=dx, dy=dy):
+            pl.semaphore_signal(barrier, inc=1, device_id=(ix + dx, iy + dy), device_id_type=MESH)
+    near_x = has[(-1, 0)].astype(jnp.int32) + has[(1, 0)].astype(jnp.int32)
+    near_y = has[(0, -1)].astype(jnp.int32) + has[(0, 1)].astype(jnp.int32)
+    pl.semaphore_wait(barrier, gx + gy - 2 + near_x * near_y)
 
     groups = rows // 8
     tile_lane = lane[0:8]
@@ -310,34 +313,81 @@
             total = total + x(c) * y(c)
         return jnp.sum(total, axis=0, keepdims=True)
 
-    def part_copy(n, d):
-        target = lax.rem(me + d, count)
-        return pltpu.make_async_remote_copy(
-            src_ref=sred.at[n], dst_ref=redall.at[n, me], send_sem=rsend.at[n, d - 1],
-            recv_sem=rrecv.at[n, d - 1], device_id=(lax.div(target, gy), lax.rem(target, gy)),
-            device_id_type=MESH)
-
-    def start_reduce(n, parts):
+    def line_copies(axis, src, dst, send_sems, recv_sems):
+        copies = []
+        for d in range(1, (gx, gy)[axis]):
+            if axis:
+                target = (ix, lax.rem(iy + d, gy))
+            else:
+                target = (lax.rem(ix + d, gx), iy)
+            copies.append(pltpu.make_async_remote_copy(
+                src_ref=src, dst_ref=dst.at[(ix, iy)[axis]], send_sem=send_sems.at[d - 1],
+                recv_sem=recv_sems.at[d - 1], device_id=target, device_id_type=MESH))
+        return copies
+
+    def fill(parts, n):
         sred[n] = jnp.zeros(sred.shape[1:], jnp.float32)
         for i, part in enumerate(parts):
             sred[n, i:i + 1] = part
 
-        def start(d, carry):
-            part_copy(n, d).start()
-            return carry
-
-        lax.fori_loop(1, count, start, 0)
-        redall[n, me] = sred[n]
-
-    def reduced(n):
-        def finish(d, carry):
-            part_copy(n, d).wait()
-            return carry
-
-        lax.fori_loop(1, count, finish, 0)
-        total = lax.fori_loop(1, count, lambda i, t: t + redall[n, i], redall[n, 0])
+    def finish_sum(total):
         total = jnp.sum(total, axis=1, keepdims=True)
         return total[0:1], total[1:2], total[2:3]
+
+    def start_lines(parts):
+        fill(parts, 0)
+        copies = line_copies(1, sred.at[0], redy, ysend, yrecv)
+        for copy in copies:
+            copy.start()
+        redy[iy] = sred[0]
+        return copies
+
+    def turn_lines(copies):
+        for copy in copies:
+            copy.wait()
+        total = redy[0]
+        for i in range(1, gy):
+            total = total + redy[i]
+        sred[1] = total
+        copies = line_copies(0, sred.at[1], redx, xsend, xrecv)
+        for copy in copies:
+            copy.start()
+        redx[ix] = total
+        return copies
+
+    def end_lines(copies):
+        for copy in copies:
+            copy.wait()
+        total = redx[0]
+        for i in range(1, gx):
+            total = total + redx[i]
+        return finish_sum(total)
+
+    def part_copy(d):
+        target = lax.rem(me + d, count)
+        return pltpu.make_async_remote_copy(
+            src_ref=sred.at[2], dst_ref=redall.at[me], send_sem=rsend.at[d - 1],
+            recv_sem=rrecv.at[d - 1], device_id=(lax.div(target, gy), lax.rem(target, gy)),
+            device_id_type=MESH)
+
+    def reduce_all(parts):
+        fill(parts, 2)
+
+        def start(d, carry):
+            part_copy(d).start()
+            return carry
+
+        def finish(d, carry):
+            part_copy(d).wait()
+            return carry
+
+        lax.fori_loop(1, count, start, 0)
+        redall[me] = sred[2]
+        lax.fori_loop(1, count, finish, 0)
+        total = redall[0]
+        for i in range(1, count):
+            total = total + redall[i]
+        return finish_sum(total)
 
     precondition(vb, z1)
     loads[7].wait()
@@ -358,7 +408,7 @@
     for n, (dx, dy) in enumerate(CORNERS):
         send(24 + n, sfp.at[(1 + dy) // 2], rfd.at[3 - n], dx, dy)
     group = sent[mark:]
-    start_reduce(0, [
+    copies = start_lines([
         dot(lambda c: vb[c], lambda c: vb[c]),
         dot(lambda c: vb[c], lambda c: w1[c]),
         dot(lambda c: w1[c], lambda c: w1[c]),
@@ -371,9 +421,10 @@
         fext[block * rows:(block + 1) * rows, 0:cols] = own
         fext[block * rows:(block + 1) * rows, cols:2 * cols] = unpack(left, right, 0.0)
     precondition(w1, q1)
+    copies = turn_lines(copies)
     operate(2, q1, vout)
 
-    bb, bw, ww = reduced(0)
+    bb, bw, ww = end_lines(copies)
     beta = jnp.sqrt(bb)
     h11 = bw / bb
     h21 = jnp.sqrt(ww / bb - h11 * h11)
@@ -386,12 +437,11 @@
     def basis2(c):
         return (w1[c] - h11 * vb[c]) * scale
 
-    start_reduce(1, [
+    h12, h22, squared = reduce_all([
         dot(mapped, lambda c: vb[c] * over),
         dot(mapped, basis2),
         dot(mapped, mapped),
     ])
-    h12, h22, squared = reduced(1)
     h32 = jnp.sqrt(squared - h12 * h12 - h22 * h22)
 
     radius1 = jnp.sqrt(h11 * h11 + h21 * h21)
@@ -439,8 +489,9 @@
             vm(4, 8, cols),
             vm(5, *wide), vm(4, *wide), vm(4, *wide), vm(4, *wide), vm(4, *wide),
             vm(4, *wide), vm(3, *wide), vm(*wide), vm(*field),
-            vm(2, 8, cols), vm(2, gx * gy, 8, cols),
-            dma(8), dma(28), dma(28), dma(2, gx * gy - 1), dma(2, gx * gy - 1),
+            vm(3, 8, cols), vm(gy, 8, cols), vm(gx, 8, cols), vm(gx * gy, 8, cols),
+            dma(8), dma(28), dma(28), dma(gy - 1), dma(gy - 1), dma(gx - 1), dma(gx - 1),
+            dma(gx * gy - 1), dma(gx * gy - 1),
         ],
         compiler_params=pltpu.CompilerParams(
             collective_id=0, has_side_effects=True, vmem_limit_bytes=60 << 20),

time: 43.1 us -> 41.8 us (0.970)
  Pallas kernels: 39 us -> 37.7 us
    pallas_call x1, Pallas kernels: 39 us -> 37.7 us  [on_device(): pl.pallas_call(functools.partial(kernel, gx, gy), name='cpr_gmres', out_s...]
where the time goes in v4:
time: 41.8 us; the launch traced here: 41.7 us
  Pallas kernels  37.7 us (90%)
  between operations  2.39 us (6%)
  local copies, waits for them, and re-layouts  1.58 us (4%)
    pallas_call x1, Pallas kernels, on_device(): pl.pallas_call(functools.partial(kernel, gx, gy), name='cpr_gmres', out_s...  37.7 us
    unnamed x1, local copies, waits for them, and re-layouts  1.58 us

profile of v4, /device:TPU:0, one launch (start us, length us, event | category | flops | bytes accessed | tf_op | source)
XLA Modules:
  0.0 41.7 jit_solution(6030805809904343844)
XLA Ops:
  0.6 37.7 %cpr_gmres.1 = (f32[9,32,128]{2,1,0:T(8,128)}, f32[1,1]{1,0:T(1,128)}) custom-call(f32[9,32,128]{2,1,0:T(8,128)} %b_hbm.1, f32[9,9,32,128]{3,2,1,0:T(8,128)} %diag_hbm.1, f32[9,9,32,128]{3,2,1,0:T(8,128)} %couple_hbm.1, f32[4,32,128]{2,1,0:T(8,128)} %trans_hbm.1, f32[9,32,128]{2,1,0:T(8,128)} %weights_hbm.1, s32[32,128]{1,0:T(8,128)} %well_hbm.1), custom_call_target="tpu_custom_call" | custom-call | tf_op jit(solution)/shard_map/cpr_gmres/pallas_call | solution.py:476
  38.3 1.6 %copy.10 = f32[9,32,128]{2,1,0:T(8,128)} copy(f32[9,32,128]{2,1,0:T(8,128)} %get-tuple-element.8) | data formatting | bytes 294912

commit v5 on v4

--- a/solution.py
+++ b/solution.py
@@ -24,7 +24,7 @@
 
 def kernel(gx, gy, b_hbm, diag_hbm, couple_hbm, trans_hbm, weights_hbm, well_hbm, out_hbm, est_ref,
            vb, vd, vc, vt, vw, vwell, inv, coup, prod, z1, w1, q1, srow, rrow, scol, rcol,
-           sown, spack, rx, ry, rd, sf, sfp, rfx, rfy, rfd, ext, link0, scaled0, link1, scaled1,
+           sown, spack, rx, ry, rd, sf, sfp, sfix, rfix, lown, rfx, rfy, rfd, ext, link0, scaled0, link1, scaled1,
            scaled2, recip, fext, vout, sred, redy, redx, redall,
            in_sem, ssem, rsem, ysend, yrecv, xsend, xrecv, rsend, rrecv):
     nc, rows, cols = vb.shape
@@ -63,6 +63,8 @@
         for r in range(3):
             rrow[r, s] = jnp.zeros(rrow.shape[2:], jnp.float32)
             rcol[r, s] = zero
+    for s in range(8):
+        rfix[s] = blank
     for s in range(4):
         for i in range(6):
             rd[s, i] = blank + 1.0 if i == 0 else blank
@@ -159,13 +161,16 @@
         rhs = rhs + vw[c] * vb[c]
     sown[0] = center
     sown[5] = rhs
-    receive(group)
+    first_edges = group
     links = [zero] * 4
     for c in range(nc):
-        for d, value in enumerate(neighbours(0, c, vc[c, 0])):
-            value = vt[d] * value
-            coup[d, c] = value
-            links[d] = links[d] - vw[c] * value
+        value = vc[c, 0]
+        shifted = (jnp.where(row == rows - 1, 0.0, roll(value, -1, 0)),
+                   jnp.where(row == 0, 0.0, roll(value, 1, 0)),
+                   jnp.where(lane == cols - 1, 0.0, roll(value, -1, 1)),
+                   jnp.where(lane == 0, 0.0, roll(value, 1, 1)))
+        for d in range(4):
+            links[d] = links[d] - vw[c] * (vt[d] * shifted[d])
     for d in range(4):
         sown[1 + d] = links[d]
 
@@ -181,6 +186,27 @@
     for n, (dx, dy) in enumerate(CORNERS):
         send(16 + n, spack.at[(1 + dy) // 2], rd.at[3 - n], dx, dy)
     group = sent[mark:]
+
+    receive(first_edges)
+    links = [zero] * 4
+    for c in range(nc):
+        for d, value in enumerate(neighbours(0, c, vc[c, 0])):
+            value = vt[d] * value
+            coup[d, c] = value
+            links[d] = links[d] - vw[c] * value
+    for d in range(4):
+        lown[d] = links[d]
+    sfix[...] = blank
+    sfix[0:1] = links[0][rows - 1:rows]
+    sfix[1:2] = links[1][0:1]
+    for d, at in ((2, cols - 1), (3, 0)):
+        spread = jnp.broadcast_to(links[d][:, at:at + 1], (rows, cols))
+        sfix[d:d + 1] = jnp.sum(jnp.where(row == lane, spread, 0.0), axis=0, keepdims=True)
+    mark = len(sent)
+    for n, (dx, dy) in enumerate(SIDES + CORNERS):
+        slot = n ^ 1 if n < 4 else 11 - n
+        send(28 + n, sfix, rfix.at[slot], dx, dy)
+    fixes = sent[mark:]
 
     loads[6].wait()
     for c in range(1, nc):
@@ -208,14 +234,30 @@
 
     lax.fori_loop(0, rows // 8, invert, 0)
     receive(group)
+    receive(fixes)
+
+    def column(slot, d):
+        return jnp.sum(jnp.where(row == lane, rfix[slot, d:d + 1], 0.0), axis=1, keepdims=True)
+
+    def mend(d, plane, left, right):
+        if d < 2:
+            edge = jnp.where(lane[0:1] < cols // 2, rfix[right, d:d + 1], rfix[left, d:d + 1])
+            return jnp.where(row == (rows - 1, 0)[d], edge, plane)
+        slot, at = ((left, cols - 1), (right, 0))[d - 2]
+        return jnp.where(lane == at, column(slot, d), plane)
 
     for i in range(6):
         fill = 1.0 if i == 0 else 0.0
         for block in range(3):
-            own = (rx[0, i], sown[i], rx[1, i])[block]
+            border = 1 <= i <= 4
+            own = (rx[0, i], lown[i - 1] if border else sown[i], rx[1, i])[block]
+            if border and block != 1:
+                own = mend(i - 1, own, block // 2, block // 2)
             left = (rd[0, i], ry[0, i], rd[2, i])[block]
             right = (rd[1, i], ry[1, i], rd[3, i])[block]
             halo = unpack(left, right, fill)
+            if border:
+                halo = mend(i - 1, halo, (4, 2, 6)[block], (5, 3, 7)[block])
             target = fext if i == 5 else ext.at[i]
             target[block * rows:(block + 1) * rows, 0:cols] = own
             target[block * rows:(block + 1) * rows, cols:2 * cols] = halo
@@ -485,12 +527,13 @@
             vm(*field), vm(*field), vm(*field), vm(*field),
             vm(3, 2, pad, cols), vm(3, 2, pad, cols), vm(3, 2, rows, cols), vm(3, 2, rows, cols),
             vm(6, rows, cols), vm(2, 6, 8, cols), vm(2, 6, rows, cols), vm(2, 6, 8, cols),
-            vm(4, 6, 8, cols), vm(rows, cols), vm(2, 8, cols), vm(2, rows, cols), vm(2, 8, cols),
+            vm(4, 6, 8, cols), vm(rows, cols), vm(2, 8, cols), vm(8, cols), vm(8, 8, cols),
+            vm(4, rows, cols), vm(2, rows, cols), vm(2, 8, cols),
             vm(4, 8, cols),
             vm(5, *wide), vm(4, *wide), vm(4, *wide), vm(4, *wide), vm(4, *wide),
             vm(4, *wide), vm(3, *wide), vm(*wide), vm(*field),
             vm(3, 8, cols), vm(gy, 8, cols), vm(gx, 8, cols), vm(gx * gy, 8, cols),
-            dma(8), dma(28), dma(28), dma(gy - 1), dma(gy - 1), dma(gx - 1), dma(gx - 1),
+            dma(8), dma(36), dma(36), dma(gy - 1), dma(gy - 1), dma(gx - 1), dma(gx - 1),
             dma(gx * gy - 1), dma(gx * gy - 1),
         ],
         compiler_params=pltpu.CompilerParams(

time: 41.8 us -> 40.7 us (0.974)
  Pallas kernels: 37.7 us -> 36.6 us
    pallas_call x1, Pallas kernels: 37.7 us -> 36.6 us  [on_device(): pl.pallas_call(functools.partial(kernel, gx, gy), name='cpr_gmres', out_s...]
where the time goes in v5:
time: 40.7 us; the launch traced here: 40.5 us
  Pallas kernels  36.6 us (90%)
  between operations  2.39 us (6%)
  local copies, waits for them, and re-layouts  1.58 us (4%)
    pallas_call x1, Pallas kernels, on_device(): pl.pallas_call(functools.partial(kernel, gx, gy), name='cpr_gmres', out_s...  36.6 us
    unnamed x1, local copies, waits for them, and re-layouts  1.58 us

profile of v5, /device:TPU:0, one launch (start us, length us, event | category | flops | bytes accessed | tf_op | source)
XLA Modules:
  0.0 40.5 jit_solution(16741215108237049142)
XLA Ops:
  0.6 36.6 %cpr_gmres.1 = (f32[9,32,128]{2,1,0:T(8,128)}, f32[1,1]{1,0:T(1,128)}) custom-call(f32[9,32,128]{2,1,0:T(8,128)} %b_hbm.1, f32[9,9,32,128]{3,2,1,0:T(8,128)} %diag_hbm.1, f32[9,9,32,128]{3,2,1,0:T(8,128)} %couple_hbm.1, f32[4,32,128]{2,1,0:T(8,128)} %trans_hbm.1, f32[9,32,128]{2,1,0:T(8,128)} %weights_hbm.1, s32[32,128]{1,0:T(8,128)} %well_hbm.1), custom_call_target="tpu_custom_call" | custom-call | tf_op jit(solution)/shard_map/cpr_gmres/pallas_call | solution.py:518
  37.2 1.6 %copy.10 = f32[9,32,128]{2,1,0:T(8,128)} copy(f32[9,32,128]{2,1,0:T(8,128)} %get-tuple-element.8) | data formatting | bytes 294912
